TPU v7x, 256 devices: a whole 4x4x8 slice. The times are simulated.
256 devices in a mesh: outer: 8 (over z), inner: 32 (over y, x, core).
Axes of the slice: x: 4, y: 4, z: 8, core: 2. Of those that a mesh axis runs over, the one named last changes fastest.
Arguments:
- context: bfloat16 [32768, 4096], P(('outer', 'inner')), may hold values from -5 to 5
- query_acts: bfloat16 [64, 4096], replicated, may hold values from -5 to 5
- norm_gain: float32 [4096], replicated, may hold values from 0.25 to 1.75
- w_query: bfloat16 [4096, 2048], P('inner'), may hold values from -0.078125 to 0.078125
- w_key: bfloat16 [4096, 512], P('inner'), may hold values from -0.453125 to 0.453125
- value_weight: bfloat16 [4096, 512], P('inner'), may hold values from -0.09375 to 0.09375
- lengths: int32 [256], replicated, may hold values from 64 to 128, as said below
Outputs:
- block_out: bfloat16 [32768, 2048], P(('outer', 'inner'))
- query_out: bfloat16 [64, 2048], replicated
Inputs may be any that keep to these rules, and one draw needn't show every extreme that they name: `lengths`: valid tokens of a block are its first ones; the rest of it is padding.
All inputs are finite; a program needn't handle non-finite values.
Results may differ from a plain program's by a relative error of at most 0.004.
The roundings to bfloat16 on the way count: a program that leaves them out, or rounds other values in their place, can miss the bound.
Values may be sent and summed in bfloat16 or wider, within the bound.
No kernel may reach another device: no remote copies, remote signals or barrier semaphores. Data moves between devices by JAX's collectives and lax.ppermute only.
A program may use at most 320 MiB of HBM per device.

v0:
```python
import jax
import jax.numpy as jnp
from jax import lax
from jax.sharding import PartitionSpec as P

QUERY_HEADS = 16
KEY_VALUE_HEADS = 4
HEAD_SIZE = 128
epsilon = 1e-05


def broadcast(block, axis, owner):
    block = jnp.where(lax.axis_index(axis) == owner, block, jnp.zeros_like(block))
    return lax.psum(block, axis)


def normalize(matrix, norm_gain):
    widened = matrix.astype(jnp.float32)
    factor = lax.rsqrt(jnp.mean(widened * widened, axis=-1, keepdims=True) + epsilon)
    return (widened * factor * norm_gain).astype(jnp.bfloat16)


def attend_part(query_rows, key_row_block, value_matrix, allowed):
    count_of_rows = query_rows.shape[0]
    head_groups = query_rows.reshape(
        count_of_rows, KEY_VALUE_HEADS, QUERY_HEADS // KEY_VALUE_HEADS, HEAD_SIZE
    )
    per_head_keys = key_row_block.reshape(key_row_block.shape[0], KEY_VALUE_HEADS, HEAD_SIZE)
    per_head_values = value_matrix.reshape(value_matrix.shape[0], KEY_VALUE_HEADS, HEAD_SIZE)
    scores = jnp.einsum(
        "rhgd,khd->hgrk", head_groups, per_head_keys, preferred_element_type=jnp.float32
    ) * HEAD_SIZE ** (-0.5)
    scores = jnp.where(allowed, scores, -jnp.inf)
    maxima = jnp.max(scores, axis=-1)
    weights = jnp.exp(scores - maxima[..., None])
    sum_exp = jnp.sum(weights, axis=-1)
    numerator = jnp.einsum(
        "hgrk,khd->rhgd",
        weights.astype(jnp.bfloat16),
        per_head_values,
        preferred_element_type=jnp.float32,
    )
    return (
        maxima.reshape(QUERY_HEADS, count_of_rows),
        sum_exp.reshape(QUERY_HEADS, count_of_rows),
        numerator.reshape(count_of_rows, QUERY_HEADS * HEAD_SIZE),
    )


def spread(factor):
    return jnp.repeat(factor.T, HEAD_SIZE, axis=1)


def combine(former, latter):
    maxima = jnp.maximum(former[0], latter[0])
    scale_one = jnp.exp(former[0] - maxima)
    scale_two = jnp.exp(latter[0] - maxima)
    return (
        maxima,
        former[1] * scale_one + latter[1] * scale_two,
        former[2] * spread(scale_one) + latter[2] * spread(scale_two),
    )


def finish(pieces):
    return (pieces[2] / spread(pieces[1])).astype(jnp.bfloat16)


def share_anchor(stacked):
    return broadcast(stacked, ("outer", "inner"), 0)


def per_device(context, query_acts, norm_gain, w_query, w_key, value_weight, lengths):
    block_rows = context.shape[0]
    normed = jnp.concatenate(
        [normalize(context, norm_gain), normalize(query_acts, norm_gain)], axis=0
    )

    def apply_weight(whole_weight):
        return jnp.dot(normed, whole_weight, preferred_element_type=jnp.float32).astype(
            jnp.bfloat16
        )

    whole_q, whole_k, whole_v = (
        lax.all_gather(w_query, "inner", axis=0, tiled=True),
        lax.all_gather(w_key, "inner", axis=0, tiled=True),
        lax.all_gather(value_weight, "inner", axis=0, tiled=True),
    )
    projected_k = apply_weight(whole_k)
    projected_v = apply_weight(whole_v)
    anchor = share_anchor(jnp.stack([projected_k[:block_rows], projected_v[:block_rows]]))
    projected_q = apply_weight(whole_q)
    position = lax.axis_index(("outer", "inner"))
    own_length = lengths[position]
    anchor_length = lengths[0]
    places = jnp.arange(block_rows, dtype=jnp.int32)
    causal = places[:, None] >= places[None, :]
    block_q = projected_q[:block_rows]
    block_k = projected_k[:block_rows]
    block_v = projected_v[:block_rows]
    query_q = projected_q[block_rows:]
    query_k = projected_k[block_rows:]
    query_v = projected_v[block_rows:]
    query_count = query_q.shape[0]
    own_allowed = causal & (places[None, :] < own_length)
    anchor_allowed = jnp.broadcast_to(
        (places[None, :] < anchor_length) & (position > 0), (block_rows, block_rows)
    )
    allowed = jnp.concatenate([anchor_allowed, own_allowed], axis=1)
    key_row_block = jnp.concatenate([anchor[0], block_k], axis=0)
    value_rows = jnp.concatenate([anchor[1], block_v], axis=0)
    block_out = finish(attend_part(block_q, key_row_block, value_rows, allowed))
    reached = jnp.broadcast_to(places[None, :] < own_length, (query_count, block_rows))
    block_part = attend_part(query_q, block_k, block_v, reached)
    highest = lax.pmax(block_part[0], ("outer", "inner"))
    rescale = jnp.exp(block_part[0] - highest)
    summed_parts = lax.psum(
        (block_part[1] * rescale, block_part[2] * spread(rescale)), ("outer", "inner")
    )
    merged = (highest, summed_parts[0], summed_parts[1])
    query_places = jnp.arange(query_count, dtype=jnp.int32)
    self_part = attend_part(
        query_q, query_k, query_v, query_places[:, None] >= query_places[None, :]
    )
    return (block_out, finish(combine(merged, self_part)))


def solution(mesh):
    in_specs = (
        P(("outer", "inner"), None),
        P(),
        P(),
        P("inner", None),
        P("inner", None),
        P("inner", None),
        P(),
    )
    out_specs = (P(("outer", "inner"), None), P())
    return jax.shard_map(
        per_device, mesh=mesh, in_specs=in_specs, out_specs=out_specs, check_vma=False
    )
```

profile of v0, /device:TPU:2, one launch (start us, length us, event | category | flops | bytes accessed | tf_op | source)
XLA Modules:
  0.0 875.9 jit_solution(4082930749184454192)
XLA Ops:
  7.2 0.7 all-gather.4.cloned.1.call-update
  8.0 0.7 all-gather.6.cloned.1.call-update
  8.7 0.0 all-reduce.3.cloned.1.call-start
  8.7 1.2 fusion.9
  10.0 1.5 fusion
  11.5 0.9 fusion.11
  12.5 0.3 fusion.2
  12.8 51.5 %all-gather.4.cloned.1.call-done = bf16[4096,512]{1,0:T(8,128)(2,1)} async-done(((bf16[128,512]{1,0:T(8,128)(2,1)}), bf16[4096,512]{1,0:T(8,128)(2,1)}) %all-gather.4.cloned.1.call-update) | async-done | bytes 4194320 | tf_op jit(solution)/shard_map/all_gather | solution.py:86
  64.3 3.2 convolution_convert_fusion.2
  67.6 49.9 %all-gather.6.cloned.1.call-done = bf16[4096,512]{1,0:T(8,128)(2,1)} async-done(((bf16[128,512]{1,0:T(8,128)(2,1)}), bf16[4096,512]{1,0:T(8,128)(2,1)}) %all-gather.6.cloned.1.call-update) | async-done | bytes 4194320 | tf_op jit(solution)/shard_map/all_gather | solution.py:87
  117.5 3.2 convolution_convert_fusion.1
  120.7 0.7 maximum_select_fusion
  121.4 0.0 all-gather.8.cloned.1.call-start
  121.5 0.5 all-gather.8.cloned.1.call-update
  122.0 0.0 all-reduce.5.cloned.1.call-start
  122.1 0.6 fusion.52
  122.7 0.6 compare_and_fusion
  123.2 0.6 iota_compare_fusion.2
  123.8 0.1 fusion.37
  123.9 0.1 pad_add_fusion
  124.1 0.8 copy.28
  124.9 0.7 concatenate.28
  125.6 0.6 reshape.106
  126.2 0.6 reshape.109
  126.9 246.7 %all-reduce.3.cloned.1.call-done = bf16[2,128,512]{2,1,0:T(8,128)(2,1)} async-done(((bf16[2,128,512]{2,1,0:T(8,128)(2,1)}), bf16[2,128,512]{2,1,0:T(8,128)(2,1)}) %all-reduce.3.cloned.1.call-update) | async-done | bytes 262160 | tf_op jit(solution)/shard_map/psum | solution.py:14
  373.5 1.0 fusion.49
  374.6 0.8 copy.56
  375.4 76.8 %all-gather.8.cloned.1.call-done = bf16[4096,2048]{1,0:T(8,128)(2,1)} async-done(((bf16[128,2048]{1,0:T(8,128)(2,1)}), bf16[4096,2048]{1,0:T(8,128)(2,1)}) %all-gather.8.cloned.1.call-update) | async-done | bytes 16777232 | tf_op jit(solution)/shard_map/all_gather | solution.py:85
  452.2 7.7 convolution_convert_fusion
  459.9 0.4 reshape.98
  460.3 0.5 fusion.53
  460.8 0.3 fusion.3
  461.1 0.1 copy-done.5
  461.2 0.1 copy-done.6
  461.2 0.5 fusion.12
  461.8 0.3 copy.34
  462.1 0.1 copy.33
  462.2 0.2 reshape.102
  462.4 0.3 copy-done.9
  462.7 0.4 fusion.54
  463.1 76.0 %pmax.7 = f32[16,64]{1,0:T(8,128)S(1)} all-reduce(f32[16,64]{1,0:T(8,128)S(1)} %bitcast.97), channel_id=1, replica_groups=mesh['outer'=8,'inner'=32] {'outer','inner'}, use_global_device_ids=true, to_apply=%region_6.7 | all-reduce | flops 1024 | bytes 8192 | tf_op jit(solution)/shard_map/pmax | solution.py:115
  539.1 0.4 fusion.19
  539.5 74.4 %psum.23 = f32[16,64]{1,0:T(8,128)S(1)} all-reduce(f32[16,64]{1,0:T(8,128)S(1)} %get-tuple-element.13), channel_id=1, replica_groups=mesh['outer'=8,'inner'=32] {'outer','inner'}, use_global_device_ids=true, to_apply=%region_10.11 | all-reduce | flops 1024 | bytes 8192 | tf_op jit(solution)/shard_map/psum | solution.py:117
  614.0 0.4 fusion.55
  614.4 0.1 fusion.21
  614.5 0.1 copy.47
  614.6 0.3 convolution_bitcast_fusion
  614.9 0.3 copy.45
  615.2 0.2 reshape.110
  615.4 0.1 copy.46
  615.5 0.3 convolution_bitcast_fusion.1
  615.8 0.3 copy.38
  616.2 0.2 reshape.103
  616.4 0.1 copy.39
  616.5 0.2 broadcast_in_dim.71
  616.7 1.0 bitcast_multiply_fusion.2
  617.7 0.1 copy.42
  617.8 0.3 broadcast_in_dim.68
  618.2 1.2 fusion.14
  619.3 247.2 %all-reduce.5.cloned.1.call-done = f32[64,2048]{1,0:T(8,128)} async-done(((f32[64,2048]{1,0:T(8,128)}), f32[64,2048]{1,0:T(8,128)}) %all-reduce.5.cloned.1.call-update) | async-done | bytes 524304 | tf_op jit(solution)/shard_map/psum | solution.py:117
  866.5 0.2 broadcast_in_dim.76
  866.7 0.2 broadcast_in_dim.75
  866.9 0.2 broadcast_in_dim.74
  867.1 2.2 fusion.16
  (42 shorter events, 0.4 us)
Async XLA Ops:
  7.2 4.4 copy-start.1
  7.2 5.3 copy-start
  7.2 5.3 copy-start.10
  7.2 57.1 %all-gather.4.cloned.1.call-start = ((), (), s32[]{:S(2)}) async-start(), calls=%async_computation | async-start | bytes 4325376 | tf_op jit(solution)/shard_map/all_gather | solution.py:86
  7.9 109.5 %all-gather.6.cloned.1.call-start = ((), (), s32[]{:S(2)}) async-start(), calls=%async_computation.1 | async-start | bytes 4325376 | tf_op jit(solution)/shard_map/all_gather | solution.py:87
  8.7 364.9 %all-reduce.3.cloned.1.call-start = ((), (), s32[]{:S(2)}) async-start(), calls=%async_computation.2 | async-start | bytes 524288 | tf_op jit(solution)/shard_map/psum | solution.py:14
  12.5 105.0 %copy-start.3 = (bf16[64,4096]{1,0:T(8,128)(2,1)}, bf16[64,4096]{1,0:T(8,128)(2,1)S(1)}, u32[]{:S(2)}) copy-start(bf16[64,4096]{1,0:T(8,128)(2,1)S(1)} %fusion.11) | copy-start | bytes 1572868
  67.6 54.5 %copy-start.11 = (s32[256]{0:T(256)S(1)}, s32[256]{0:T(256)}, u32[]{:S(2)}) copy-start(s32[256]{0:T(256)} %param.13) | copy-start | bytes 3076
  120.6 331.5 %copy-start.4 = (bf16[64,4096]{1,0:T(8,128)(2,1)S(1)}, bf16[64,4096]{1,0:T(8,128)(2,1)}, u32[]{:S(2)}) copy-start(bf16[64,4096]{1,0:T(8,128)(2,1)} %copy-done.3) | copy-start | bytes 1572868
  121.4 330.7 %all-gather.8.cloned.1.call-start = ((), (), s32[]{:S(2)}) async-start(), calls=%async_computation.3 | async-start | bytes 17301504 | tf_op jit(solution)/shard_map/all_gather | solution.py:85
  122.0 744.5 %all-reduce.5.cloned.1.call-start = ((), (), s32[]{:S(2)}) async-start(), calls=%async_computation.4 | async-start | bytes 1048576 | tf_op jit(solution)/shard_map/psum | solution.py:117
  459.8 0.9 copy-start.2
  460.3 0.9 copy-start.5
  460.3 1.0 copy-start.6
  461.2 1.0 slice-start
  461.7 0.9 copy-start.9
  461.8 152.2 %copy-start.8 = (bf16[64,4,128]{2,1,0:T(4,128)(2,1)S(1)}, bf16[64,4,128]{2,1,0:T(4,128)(2,1)}, u32[]{:S(2)}) copy-start(bf16[64,4,128]{2,1,0:T(4,128)(2,1)} %reshape.106) | copy-start | bytes 196612
  462.1 152.5 %copy-start.7 = (bf16[64,4,128]{2,1,0:T(4,128)(2,1)S(1)}, bf16[64,4,128]{2,1,0:T(4,128)(2,1)}, u32[]{:S(2)}) copy-start(bf16[64,4,128]{2,1,0:T(4,128)(2,1)} %reshape.109) | copy-start | bytes 196612
Sparse Core Ops, SparseCore 0:
  10.6 53.7 all-gather.3
  66.9 50.5 all-gather.5
  123.5 250.0 all-reduce.2
  375.9 76.1 all-gather.7
  617.9 248.6 all-reduce.4
where the time goes:
time: 876 us
  waiting for transfers between devices  674 us (77%)
  blocking collectives  150 us (17%)
  matrix products  16.3 us (2%)
  between operations  14.2 us (2%)
  other arithmetic  11.4 us (1%)
  local copies, waits for them, and re-layouts  9.33 us (1%)
    psum x1, waiting for transfers between devices, per_device(): lax.psum((block_part[1] * rescale, block_part[2] * spread(rescale)), ('ou...  247 us
    psum x1, waiting for transfers between devices, broadcast(): return lax.psum(block, axis)  247 us
    all_gather x1, waiting for transfers between devices, per_device(): lax.all_gather(w_query, 'inner', axis=0, tiled=True)  76.8 us
    pmax x1, blocking collectives, per_device(): highest = lax.pmax(block_part[0], ('outer', 'inner'))  76 us
    psum x1, blocking collectives, per_device(): lax.psum((block_part[1] * rescale, block_part[2] * spread(rescale)), ('ou...  74.4 us
    all_gather x1, waiting for transfers between devices, per_device(): lax.all_gather(w_key, 'inner', axis=0, tiled=True)  51.5 us
    all_gather x1, waiting for transfers between devices, per_device(): lax.all_gather(value_weight, 'inner', axis=0, tiled=True)  49.9 us
  transfers between devices with their start and end apart: 5, of which 5 were waited for; matrix products, arithmetic and copies ran while one was open for 2% of the time, Pallas kernels for 0%

commit v1 on v0

--- a/solution.py
+++ b/solution.py
@@ -11,7 +11,7 @@
 
 def broadcast(block, axis, owner):
     block = jnp.where(lax.axis_index(axis) == owner, block, jnp.zeros_like(block))
-    return lax.psum(block, axis)
+    return jnp.sum(lax.all_gather(block, axis), axis=0)
 
 
 def normalize(matrix, norm_gain):

time: 876 us -> 782 us (0.89)
  waiting for transfers between devices: 674 us -> 560 us
  other arithmetic: 11.4 us -> 32.1 us
    psum x1 -> x0, waiting for transfers between devices: 247 us -> none  [broadcast(): return lax.psum(block, axis)]
    all_gather x0 -> x1, waiting for transfers between devices: none -> 212 us  [broadcast(): return jnp.sum(lax.all_gather(block, axis), axis=0)]
    psum x1, waiting for transfers between devices: 247 us -> 171 us  [per_device(): lax.psum((block_part[1] * rescale, block_part[2] * spread(rescale)), ('ou...]
    reduce_sum x0 -> x1, other arithmetic: none -> 21.3 us  [broadcast(): return jnp.sum(lax.all_gather(block, axis), axis=0)]
where the time goes in v1:
time: 782 us; the launch traced here: 780 us
  waiting for transfers between devices  560 us (72%)
  blocking collectives  151 us (19%)
  other arithmetic  32.1 us (4%)
  matrix products  16.5 us (2%)
  between operations  14.2 us (2%)
    all_gather x1, waiting for transfers between devices, broadcast(): return jnp.sum(lax.all_gather(block, axis), axis=0)  212 us
    psum x1, waiting for transfers between devices, per_device(): lax.psum((block_part[1] * rescale, block_part[2] * spread(rescale)), ('ou...  171 us
    all_gather x1, waiting for transfers between devices, per_device(): lax.all_gather(w_query, 'inner', axis=0, tiled=True)  76.4 us
    pmax x1, blocking collectives, per_device(): highest = lax.pmax(block_part[0], ('outer', 'inner'))  76 us
    psum x1, blocking collectives, per_device(): lax.psum((block_part[1] * rescale, block_part[2] * spread(rescale)), ('ou...  75.2 us
    all_gather x1, waiting for transfers between devices, per_device(): lax.all_gather(w_key, 'inner', axis=0, tiled=True)  49.5 us
    all_gather x1, waiting for transfers between devices, per_device(): lax.all_gather(value_weight, 'inner', axis=0, tiled=True)  49.2 us
    reduce_sum x1, other arithmetic, broadcast(): return jnp.sum(lax.all_gather(block, axis), axis=0)  21.3 us
  transfers between devices with their start and end apart: 5, of which 5 were waited for; matrix products, arithmetic and copies ran while one was open for 2% of the time, Pallas kernels for 0%

profile of v1, /device:TPU:2, one launch (start us, length us, event | category | flops | bytes accessed | tf_op | source)
XLA Modules:
  0.0 780.3 jit_solution(13975303522686498026)
XLA Ops:
  7.2 0.0 all-gather.5.cloned.1.call-start
  7.2 0.7 all-gather.5.cloned.1.call-update
  7.9 0.0 all-gather.7.cloned.1.call-start
  8.0 0.7 all-gather.7.cloned.1.call-update
  8.7 0.0 all-gather.11.cloned.1.call-start
  8.7 0.7 all-gather.11.cloned.1.call-update
  9.4 0.0 all-reduce.2.cloned.1.call-start
  9.5 1.3 fusion.52
  10.8 0.6 iota_compare_fusion.2
  11.5 1.2 fusion.9
  12.7 1.5 fusion
  14.3 0.2 fusion.11
  14.5 0.3 fusion.2
  14.8 49.5 %all-gather.5.cloned.1.call-done = bf16[4096,512]{1,0:T(8,128)(2,1)} async-done(((bf16[128,512]{1,0:T(8,128)(2,1)}), bf16[4096,512]{1,0:T(8,128)(2,1)}) %all-gather.5.cloned.1.call-update) | async-done | bytes 4194320 | tf_op jit(solution)/shard_map/all_gather | solution.py:86
  64.3 3.2 convolution_convert_fusion.2
  67.5 0.7 copy-done.5
  68.3 49.2 %all-gather.7.cloned.1.call-done = bf16[4096,512]{1,0:T(8,128)(2,1)} async-done(((bf16[128,512]{1,0:T(8,128)(2,1)}), bf16[4096,512]{1,0:T(8,128)(2,1)}) %all-gather.7.cloned.1.call-update) | async-done | bytes 4194320 | tf_op jit(solution)/shard_map/all_gather | solution.py:87
  117.4 3.3 convolution_convert_fusion.1
  120.9 76.4 %all-gather.11.cloned.1.call-done = bf16[4096,2048]{1,0:T(8,128)(2,1)} async-done(((bf16[128,2048]{1,0:T(8,128)(2,1)}), bf16[4096,2048]{1,0:T(8,128)(2,1)}) %all-gather.11.cloned.1.call-update) | async-done | bytes 16777232 | tf_op jit(solution)/shard_map/all_gather | solution.py:85
  197.3 7.7 convolution_convert_fusion
  205.0 0.2 reshape.133
  205.2 0.4 fusion.54
  205.6 0.4 fusion.19
  206.0 76.0 %pmax.7 = f32[16,64]{1,0:T(8,128)S(1)} all-reduce(f32[16,64]{1,0:T(8,128)S(1)} %bitcast.99), channel_id=1, replica_groups=mesh['outer'=8,'inner'=32] {'outer','inner'}, use_global_device_ids=true, to_apply=%region_6.7 | all-reduce | flops 1024 | bytes 8192 | tf_op jit(solution)/shard_map/pmax | solution.py:115
  282.0 0.1 copy.58
  282.1 0.3 convolution_bitcast_fusion.1
  282.4 0.3 copy.57
  282.8 0.2 reshape.134
  283.0 0.2 broadcast_in_dim.71
  283.2 1.0 bitcast_multiply_fusion.2
  284.2 0.0 all-reduce.2.cloned.1.call-update
  284.3 0.0 all-gather.9.cloned.1.call-start
  284.3 0.8 maximum_select_fusion
  285.1 0.6 compare_and_fusion
  285.7 0.1 fusion.37
  285.8 0.1 pad_add_fusion
  285.9 0.1 copy.46
  286.2 75.2 %psum.15 = f32[16,64]{1,0:T(8,128)S(1)} all-reduce(f32[16,64]{1,0:T(8,128)S(1)} %get-tuple-element.13), channel_id=1, replica_groups=mesh['outer'=8,'inner'=32] {'outer','inner'}, use_global_device_ids=true, to_apply=%region_10.11 | all-reduce | flops 1024 | bytes 8192 | tf_op jit(solution)/shard_map/psum | solution.py:117
  361.4 0.4 fusion.55
  361.8 0.1 fusion.21
  362.0 0.1 copy.61
  362.1 0.1 copy.65
  362.1 0.1 copy.66
  362.2 0.3 convolution_bitcast_fusion
  362.5 0.3 copy.64
  362.9 0.2 reshape.141
  363.1 0.4 reshape.129
  363.4 170.7 %all-reduce.2.cloned.1.call-done = f32[64,2048]{1,0:T(8,128)} async-done(((f32[64,2048]{1,0:T(8,128)}), f32[64,2048]{1,0:T(8,128)}) %all-reduce.2.cloned.1.call-update) | async-done | bytes 524304 | tf_op jit(solution)/shard_map/psum | solution.py:117
  534.2 0.2 broadcast_in_dim.74
  534.4 0.2 broadcast_in_dim.75
  534.6 0.2 broadcast_in_dim.76
  534.8 2.2 fusion.16
  537.0 211.8 %all-gather.9.cloned.1.call-done = bf16[256,2,128,512]{3,2,1,0:T(8,128)(2,1)} async-done(((bf16[1,2,128,512]{3,2,1,0:T(8,128)(2,1)}), bf16[256,2,128,512]{3,2,1,0:T(8,128)(2,1)}) %all-gather.9.cloned.1.call-update) | async-done | bytes 67108880 | tf_op jit(solution)/shard_map/all_gather | solution.py:14
  748.8 21.3 %reduce_sum.59 = bf16[2,128,512]{2,1,0:T(8,128)(2,1)S(1)} reduce(bf16[256,2,128,512]{3,2,1,0:T(8,128)(2,1)} %all-gather.9.cloned.1.call-done, bf16[]{:T(256)} %constant.10.clone.1), dimensions={0}, to_apply=%region_2.3 | reduce | flops 33423360 | bytes 67371008 | tf_op jit(solution)/shard_map/reduce_sum | solution.py:14
  770.2 0.1 copy.47
  770.3 0.1 copy.48
  770.4 0.5 fusion.53
  770.9 0.3 fusion.3
  771.2 0.1 copy.52
  771.3 0.1 copy.45
  771.4 0.5 fusion.12
  771.9 0.3 copy.53
  772.3 0.3 broadcast_in_dim.68
  772.6 1.2 fusion.14
  (37 shorter events, 0.4 us)
Async XLA Ops:
  7.2 7.1 copy-start.1
  7.2 7.3 copy-start
  7.2 7.1 copy-start.7
  7.2 57.1 %all-gather.5.cloned.1.call-start = ((), (), s32[]{:S(2)}) async-start(), calls=%async_computation | async-start | bytes 4325376 | tf_op jit(solution)/shard_map/all_gather | solution.py:86
  7.9 109.5 %all-gather.7.cloned.1.call-start = ((), (), s32[]{:S(2)}) async-start(), calls=%async_computation.1 | async-start | bytes 4325376 | tf_op jit(solution)/shard_map/all_gather | solution.py:87
  8.7 188.6 %all-gather.11.cloned.1.call-start = ((), (), s32[]{:S(2)}) async-start(), calls=%async_computation.3 | async-start | bytes 17301504 | tf_op jit(solution)/shard_map/all_gather | solution.py:85
  9.4 524.7 %all-reduce.2.cloned.1.call-start = ((), (), s32[]{:S(2)}) async-start(), calls=%async_computation.4 | async-start | bytes 1048576 | tf_op jit(solution)/shard_map/psum | solution.py:117
  14.5 49.9 %copy-start.3 = (bf16[64,4096]{1,0:T(8,128)(2,1)}, bf16[64,4096]{1,0:T(8,128)(2,1)S(1)}, u32[]{:S(2)}) copy-start(bf16[64,4096]{1,0:T(8,128)(2,1)S(1)} %fusion.11) | copy-start | bytes 1572868
  67.5 0.7 copy-start.5
  68.3 129.0 %copy-start.4 = (bf16[64,4096]{1,0:T(8,128)(2,1)S(1)}, bf16[64,4096]{1,0:T(8,128)(2,1)}, u32[]{:S(2)}) copy-start(bf16[64,4096]{1,0:T(8,128)(2,1)} %copy-done.3) | copy-start | bytes 1572868
  120.8 76.5 %copy-start.6 = (bf16[192,512]{1,0:T(8,128)(2,1)}, bf16[192,512]{1,0:T(8,128)(2,1)S(1)}, u32[]{:S(2)}) copy-start(bf16[192,512]{1,0:T(8,128)(2,1)S(1)} %convolution_convert_fusion.1) | copy-start | bytes 589828
  205.0 81.2 %copy-start.2 = (bf16[192,2048]{1,0:T(8,128)(2,1)}, bf16[192,2048]{1,0:T(8,128)(2,1)S(1)}, u32[]{:S(2)}) copy-start(bf16[192,2048]{1,0:T(8,128)(2,1)S(1)} %convolution_convert_fusion) | copy-start | bytes 2359300
  283.0 3.1 slice-start.1
  283.0 3.1 slice-start.2
  284.3 464.5 %all-gather.9.cloned.1.call-start = ((), (), s32[]{:S(2)}) async-start(), calls=%async_computation.2 | async-start | bytes 67371008 | tf_op jit(solution)/shard_map/all_gather | solution.py:14
  361.8 1.2 slice-start
Sparse Core Ops, SparseCore 0:
  10.6 53.7 all-gather.4
  66.9 50.5 all-gather.6
  120.0 77.2 all-gather.10
  284.4 249.7 all-reduce.1
  537.6 211.1 all-gather.8
